TPU v7x, 32 devices: a whole 2x2x4 slice. The times are simulated.
32 devices in a mesh: grp: 2 (over x), seq: 16 (over z, y, core).
Axes of the slice: x: 2, y: 2, z: 4, core: 2. Of those that a mesh axis runs over, the one named last changes fastest.
Arguments:
- conv_input: bfloat16 [8192, 4352], P(('grp', 'seq')), parts along dimension 0, may hold values from -6 to 6, as said below
- conv_weight: float32 [4, 4352], replicated, may hold values from -3 to 3
- step_logit: float32 [8192, 32], P(('grp', 'seq')), parts along dimension 0, may hold values from -20 to 0, as said below
- decay_log: float32 [32], replicated, may hold values from -0.5 to 0.5
- skip_gain: float32 [32], replicated, may hold values from 0.5 to 2
Outputs:
- mixer_out: bfloat16 [8192, 4096], P(('grp', 'seq')), parts along dimension 0
There are 2 independent parts, one for each index of `grp`. A program takes and returns all parts, laid end to end along the dimension named above; an argument that names none is the same for every part. Nothing has to cross between parts.
Inputs may be any that keep to these rules, and one draw needn't show every extreme that they name: `conv_input`: activations before the convolution. `step_logit`: step sizes before softplus.
All inputs are finite; a program needn't handle non-finite values.
Results may differ from a plain program's by a relative error of at most 0.0047.
Values may be sent and summed in bfloat16 or wider, within the bound.
A program may use at most 128 MiB of HBM per device.

v0:
```python
import jax
import jax.numpy as jnp
from jax import lax
from jax.sharding import PartitionSpec as P

HEADDIM = 128
STATE = 128
GROUP = 256


def as_sent(shard):

    def short(part):
        return part.astype(jnp.bfloat16) if part.dtype == jnp.float32 else part

    return jax.tree.map(short, shard)


def from_behind(value, axis, steps):
    count = lax.axis_size(axis)
    leading, last = (max(0, -steps), min(count, count - steps))
    return lax.ppermute(value, axis, [(source, source + steps) for source in range(leading, last)])


def conv_activate(extended, kernel, row_count):
    running = kernel[0] * extended[0:row_count].astype(jnp.float32)
    for tap_index in range(1, kernel.shape[0]):
        running = running + kernel[tap_index] * extended[tap_index : tap_index + row_count].astype(
            jnp.float32
        )
    return jax.nn.silu(running).astype(jnp.bfloat16)


def group_terms(activated, logits, decay_rate, skip_gain):
    head_count = decay_rate.shape[0]
    inner_width = head_count * HEADDIM
    block_count = activated.shape[0]
    span_rows = activated.shape[1]
    values = activated[:, :, :inner_width].reshape(block_count, span_rows, head_count, HEADDIM)
    b_rows = activated[:, :, inner_width : inner_width + STATE]
    c_rows = activated[:, :, inner_width + STATE :]
    time_step_size = jax.nn.softplus(logits)
    cum_decay = jnp.cumsum(time_step_size * decay_rate, axis=1)
    decay_t = jnp.transpose(cum_decay, (0, 2, 1))
    step_t = jnp.transpose(time_step_size, (0, 2, 1))
    scores = jnp.einsum("cqn,csn->cqs", c_rows, b_rows, preferred_element_type=jnp.float32)
    token_position = jnp.arange(span_rows)
    causal = token_position[:, None] >= token_position[None, :]
    decay_gap = jnp.where(causal, decay_t[:, :, :, None] - decay_t[:, :, None, :], -jnp.inf)
    weights = (scores[:, None] * jnp.exp(decay_gap) * step_t[:, :, None, :]).astype(jnp.bfloat16)
    intra_out = jnp.einsum("chqs,cshp->cqhp", weights, values, preferred_element_type=jnp.float32)
    local_out = intra_out + skip_gain[:, None] * values.astype(jnp.float32)
    tail_weight = jnp.transpose(jnp.exp(decay_t[:, :, -1:] - decay_t) * step_t, (0, 2, 1))
    weighted = (values * tail_weight[..., None]).astype(jnp.bfloat16)
    states = jnp.einsum("cshp,csn->chpn", weighted, b_rows, preferred_element_type=jnp.float32)
    return (local_out, states, cum_decay, c_rows)


def split_parts(state_field):
    upper_part = lax.optimization_barrier(state_field.astype(jnp.bfloat16))
    lower_part = (state_field - upper_part.astype(jnp.float32)).astype(jnp.bfloat16)
    return (upper_part, lower_part)


def state_readout(form, c_rows, state_field):
    upper_part, lower_part = split_parts(state_field)
    upper_term = jnp.einsum(form, c_rows, upper_part, preferred_element_type=jnp.float32)
    lower_term = jnp.einsum(form, c_rows, lower_part, preferred_element_type=jnp.float32)
    return upper_term + lower_term


def chain_states(initial, group_ends, states):

    def advance(current, pieces):
        end_log, piece = pieces
        return (jnp.exp(end_log)[:, None, None] * current + piece, current)

    final_state, entering = lax.scan(advance, initial, (group_ends, states))
    return (entering, final_state)


def carry_state(device_log, final_state):
    head_count = device_log.shape[0]
    all_logs = lax.all_gather(device_log[None, :], "seq", axis=0, tiled=True)
    flat_state = final_state.reshape(1, head_count * HEADDIM, STATE)
    received = lax.all_to_all(
        flat_state.astype(jnp.bfloat16), "seq", split_axis=1, concat_axis=0, tiled=True
    ).astype(flat_state.dtype)
    source_count = received.shape[0]
    row_count = received.shape[1]
    first_row = lax.axis_index("seq") * row_count
    head_of = (first_row + jnp.arange(row_count, dtype=jnp.int32)) // HEADDIM
    head_pick = (head_of[:, None] == jnp.arange(head_count, dtype=jnp.int32)[None, :]).astype(
        jnp.float32
    )
    row_logs = jnp.dot(all_logs, head_pick.T, precision=lax.Precision.HIGHEST)
    total_log = jnp.cumsum(row_logs, axis=0)
    before_log = total_log - row_logs
    source_order = jnp.arange(source_count)
    earlier_mask = source_order[None, :] < source_order[:, None]
    exponent = jnp.where(
        earlier_mask[:, :, None], before_log[:, None, :] - total_log[None, :, :], -jnp.inf
    )
    mixed = jnp.einsum("sjr,jrn->srn", jnp.exp(exponent), received, precision=lax.Precision.HIGHEST)
    returned = lax.all_to_all(
        as_sent(mixed), "seq", split_axis=0, concat_axis=1, tiled=True
    ).astype(mixed.dtype)
    return returned.reshape(head_count, HEADDIM, STATE)


def on_device(conv_input, conv_weight, step_logit, decay_log, skip_gain):
    tap_count = conv_weight.shape[0]
    row_count = conv_input.shape[0]
    edge_rows = conv_input[row_count - (tap_count - 1) :]
    previous = from_behind(edge_rows, "seq", 1)
    extended = jnp.concatenate([previous, conv_input], 0)
    block_count = row_count // GROUP
    activated = conv_activate(extended, conv_weight, row_count).reshape(block_count, GROUP, -1)
    logits = step_logit.reshape(block_count, GROUP, -1)
    decay_rate = -jnp.exp(decay_log)
    local_out, states, cum_decay, c_rows = group_terms(activated, logits, decay_rate, skip_gain)
    group_ends = cum_decay[:, -1, :]
    device_log = jnp.sum(group_ends, axis=0)
    empty_state = jnp.zeros_like(states[0])
    _, final_state = chain_states(empty_state, group_ends, states)
    incoming = carry_state(device_log, final_state)
    entering, _ = chain_states(incoming, group_ends, states)
    inter_out = jnp.exp(cum_decay)[..., None] * state_readout("cqn,chpn->cqhp", c_rows, entering)
    result = local_out + inter_out
    return result.reshape(row_count, -1).astype(jnp.bfloat16)


def solution(mesh):
    return jax.shard_map(
        on_device,
        mesh=mesh,
        in_specs=(P(("grp", "seq"), None), P(), P(("grp", "seq"), None), P(), P()),
        out_specs=P(("grp", "seq"), None),
        check_vma=False,
    )
```

profile of v0, /device:TPU:9, one launch (start us, length us, event | category | flops | bytes accessed | tf_op | source)
XLA Modules:
  0.0 161.1 jit_solution(3897748167165078665)
XLA Ops:
  0.0 0.9 slice.46
  0.9 3.7 %collective-permute-start = (bf16[3,4352]{1,0:T(4,128)(2,1)S(1)}, bf16[3,4352]{1,0:T(4,128)(2,1)S(1)}, u32[]{:S(2)}, u32[]{:S(2)}) collective-permute-start(bf16[3,4352]{1,0:T(4,128)(2,1)S(1)} %slice.46), channel_id=1, source_target_pairs={{0,1},{1,2},{2,3},{3,4},{4,5},{5,6},{6,7},{7,8},{8,9},{9,10},{10,1... | collective-permute-start | bytes 78344 | tf_op jit(solution)/shard_map/ppermute | solution.py:22
  4.6 0.7 exponential_negate_fusion
  5.3 0.8 compare_select_fusion
  8.4 1.2 slice_reduce_fusion.4
  9.7 2.5 %mul.190 = f32[256,32,128]{2,1,0:T(8,128)} broadcast(f32[256,32]{1,0:T(8,128)S(1)} %bitcast.104), dimensions={0,1} | broadcast | bytes 4227072 | tf_op jit(solution)/shard_map/mul | solution.py:54
  12.3 5.0 %mul.191 = f32[1,256,4096]{2,1,0:T(8,128)} reshape(f32[256,32,128]{2,1,0:T(8,128)} %mul.190) | data formatting | bytes 8388608 | tf_op jit(solution)/shard_map/mul | solution.py:54
  17.3 6.1 %fusion.13 = bf16[1,256,4352]{2,1,0:T(8,128)(2,1)S(1)} fusion(bf16[256,4352]{1,0:T(8,128)(2,1)} %param.5, f32[4352]{0:T(1024)S(1)} %get-tuple-element.27, bf16[3,4352]{1,0:T(4,128)(2,1)S(1)} %collective-permute-done, f32[4352]{0:T(1024)S(1)} %get-tuple-element.28, f32[4352]{0:T(1024)S(1)} %get-tuple-element.26, f32[4352]{0:T(1024)S(1)} %get-tuple-element.20), kind=kLoop, calls=%fused_computation.21 | loop fusion | flops 27852800 | bytes 4552192 | tf_op jit(solution)/shard_map/reshape | solution.py:118
  24.5 3.0 %fusion.1 = bf16[1,4096,128]{2,1,0:T(8,128)(2,1)S(1)} fusion(bf16[32,8,32,128]{3,2,1,0:T(8,128)(2,1)S(1)} %copy.62, f32[4096]{0:T(1024)S(1)} %broadcast_bitcast_fusion, bf16[1,256,4352]{2,1,0:T(8,128)(2,1)S(1)} %fusion.13), kind=kOutput, calls=%fused_computation.3 | convolution fusion | flops 269484032 | bytes 3227648 | tf_op jit(solution)/shard_map/cshp,csn->chpn/dot_general | solution.py:55
  27.5 17.0 %copy.79 = bf16[1,4096,128]{2,0,1:T(2,128)(2,1)} copy(bf16[1,4096,128]{2,1,0:T(8,128)(2,1)S(1)} %fusion.1) | data formatting | bytes 2097152 | tf_op jit(solution)/shard_map/convert_element_type | solution.py:87
  45.1 23.7 %reduce.14 = bf16[4096,128]{1,0:T(8,128)(2,1)S(1)} reduce(bf16[4096,1,128]{2,1,0:T(2,128)(2,1)} %bitcast.99, bf16[]{:T(256)} %broadcast.138), dimensions={1}, to_apply=%bitcast.95.reduce_sub_computation | reduce | bytes 2097154
  68.8 1.1 reshape.321
  69.9 5.1 %all-to-all-start = ((bf16[16,2,16384]{2,1,0:T(2,128)(2,1)}), bf16[16,2,16384]{2,1,0:T(2,128)(2,1)S(1)}, u32[]{:S(2)}, u32[]{:S(2)}) async-start(bf16[16,2,16384]{2,1,0:T(2,128)(2,1)} %reshape.321), calls=%async_computation | async-start | bytes 2097152 | tf_op jit(solution)/shard_map/all_to_all | solution.py:86
  75.1 35.0 %all-gather = f32[16,1,32]{2,1,0:T(1,128)S(1)} all-gather(f32[1,1,32]{2,1,0:T(1,128)S(1)} %copy.49), channel_id=2, replica_groups=mesh['grp'=2,'seq'=16] {'seq'}, dimensions={0}, use_global_device_ids=true | all-gather | bytes 2176 | tf_op jit(solution)/shard_map/all_gather | solution.py:84
  111.1 1.5 copy.50
  112.5 3.4 %reshape.322 = bf16[4096,1,128]{2,1,0:T(2,128)(2,1)} reshape(bf16[16,2,16384]{2,1,0:T(2,128)(2,1)S(1)} %all-to-all-done) | data formatting | bytes 2097152
  116.0 1.7 %copy.58 = bf16[1,4096,128]{2,1,0:T(8,128)(2,1)S(1)} copy(bf16[1,4096,128]{2,0,1:T(2,128)(2,1)} %bitcast.98) | data formatting | bytes 2097152
  117.7 3.9 %fusion.24 = bf16[16,256,128]{2,0,1:T(8,128)(2,1)S(1)} fusion(bf16[16,256,128]{2,1,0:T(8,128)(2,1)S(1)} %bitcast.103, f32[16,256]{0,1:T(8,128)S(1)} %copy.51, f32[16,256]{0,1:T(8,128)} %copy.50, pred[16,16]{1,0:T(8,128)(4,1)S(1)} %iota_compare_fusion.3), kind=kOutput, calls=%fused_computation.31 | convolution fusion | flops 101318656 | bytes 2130176 | tf_op jit(solution)/shard_map/sjr,jrn->srn/dot_general | solution.py:104
  121.7 1.2 copy.53
  122.9 4.1 %all-to-all-start.1 = ((bf16[16,256,128]{2,1,0:T(8,128)(2,1)}), bf16[16,256,128]{2,1,0:T(8,128)(2,1)S(1)}, u32[]{:S(2)}, u32[]{:S(2)}) async-start(bf16[16,256,128]{2,1,0:T(8,128)(2,1)} %copy.53), calls=%async_computation.1 | async-start | bytes 2097152 | tf_op jit(solution)/shard_map/all_to_all | solution.py:105
  127.7 0.6 copy.78
  128.3 0.6 iota_compare_fusion
  129.6 3.2 %fusion.48 = (bf16[1,256,4096]{2,1,0:T(8,128)(2,1)}, f32[1,256,4096]{2,1,0:T(8,128)}) fusion(bf16[1,256,4352]{2,1,0:T(8,128)(2,1)S(1)} %fusion.13), kind=kLoop, calls=%fused_computation.80 | loop fusion | flops 1048576 | bytes 8388608 | tf_op jit(solution)/shard_map/slice | solution.py:39
  132.8 4.1 %copy.41 = bf16[1,256,4096]{1,2,0:T(8,128)(2,1)} copy(bf16[1,256,4096]{2,1,0:T(8,128)(2,1)} %get-tuple-element.36) | data formatting | bytes 4194304 | tf_op jit(solution)/shard_map/slice | solution.py:39
  136.8 5.6 %copy.45 = f32[1,256,4096]{1,2,0:T(8,128)} copy(f32[1,256,4096]{2,1,0:T(8,128)} %get-tuple-element.38) | data formatting | bytes 8388608 | tf_op jit(solution)/shard_map/convert_element_type | solution.py:52
  142.6 9.3 %all-to-all-done.1 = bf16[16,256,128]{2,1,0:T(8,128)(2,1)S(1)} async-done(((bf16[16,256,128]{2,1,0:T(8,128)(2,1)}), bf16[16,256,128]{2,1,0:T(8,128)(2,1)S(1)}, u32[]{:S(2)}, u32[]{:S(2)}) %all-to-all-start.1) | async-done | bytes 1048608 | tf_op jit(solution)/shard_map/all_to_all | solution.py:105
  152.0 0.7 fusion.28
  152.7 0.7 fusion.30
  153.4 0.7 copy-done.1
  154.1 0.7 copy-done.2
  154.8 3.4 %fusion.4 = bf16[1,256,32,128]{1,3,2,0:T(8,128)(2,1)S(1)} fusion(f32[256,32,128]{0,2,1:T(8,128)S(1)} %fusion.30, f32[256,32,128]{0,2,1:T(8,128)S(1)} %fusion.28, f32[1,256,32,128]{1,3,2,0:T(8,128)S(1)} %bitcast.100, f32[256,32]{0,1:T(8,128)S(1)} %bitcast.111, f32[32]{0:T(128)S(1)} %copy-done.7, bf16[256,32,128]{0,2,1:T(8,128)(2,1)S(1)} %bitcast.101, ...), kind=kOutput, calls=%fused_computation.8 | convolution fusion | flops 553648128 | bytes 17203328 | tf_op jit(solution)/shard_map/chqs,cshp->cqhp/dot_general | solution.py:51
  158.2 2.9 %copy.54 = bf16[256,4096]{1,0:T(8,128)(2,1)} copy(bf16[256,4096]{0,1:T(8,128)(2,1)S(1)} %bitcast.102) | data formatting | bytes 4194304 | tf_op jit(solution)/shard_map/convert_element_type | solution.py:130
  (45 shorter events, 6.6 us)
Async XLA Ops:
  0.9 16.4 %collective-permute-start = (bf16[3,4352]{1,0:T(4,128)(2,1)S(1)}, bf16[3,4352]{1,0:T(4,128)(2,1)S(1)}, u32[]{:S(2)}, u32[]{:S(2)}) collective-permute-start(bf16[3,4352]{1,0:T(4,128)(2,1)S(1)} %slice.46), channel_id=1, source_target_pairs={{0,1},{1,2},{2,3},{3,4},{4,5},{5,6},{6,7},{7,8},{8,9},{9,10},{10,1... | collective-permute-start | bytes 78344 | tf_op jit(solution)/shard_map/ppermute | solution.py:22
  17.3 6.1 %copy-start = (f32[1,256,4096]{2,1,0:T(8,128)S(1)}, f32[1,256,4096]{2,1,0:T(8,128)}, u32[]{:S(2)}) copy-start(f32[1,256,4096]{2,1,0:T(8,128)} %mul.191) | copy-start | bytes 12582916
  69.9 42.7 %all-to-all-start = ((bf16[16,2,16384]{2,1,0:T(2,128)(2,1)}), bf16[16,2,16384]{2,1,0:T(2,128)(2,1)S(1)}, u32[]{:S(2)}, u32[]{:S(2)}) async-start(bf16[16,2,16384]{2,1,0:T(2,128)(2,1)} %reshape.321), calls=%async_computation | async-start | bytes 2097152 | tf_op jit(solution)/shard_map/all_to_all | solution.py:86
  122.9 29.0 %all-to-all-start.1 = ((bf16[16,256,128]{2,1,0:T(8,128)(2,1)}), bf16[16,256,128]{2,1,0:T(8,128)(2,1)S(1)}, u32[]{:S(2)}, u32[]{:S(2)}) async-start(bf16[16,256,128]{2,1,0:T(8,128)(2,1)} %copy.53), calls=%async_computation.1 | async-start | bytes 2097152 | tf_op jit(solution)/shard_map/all_to_all | solution.py:105
  151.9 2.2 %copy-start.1 = (f32[1,256,4096]{1,2,0:T(8,128)S(1)}, f32[1,256,4096]{1,2,0:T(8,128)}, u32[]{:S(2)}) copy-start(f32[1,256,4096]{1,2,0:T(8,128)} %copy.45) | copy-start | bytes 12582916
  151.9 2.9 %copy-start.2 = (bf16[1,256,4096]{1,2,0:T(8,128)(2,1)S(1)}, bf16[1,256,4096]{1,2,0:T(8,128)(2,1)}, u32[]{:S(2)}) copy-start(bf16[1,256,4096]{1,2,0:T(8,128)(2,1)} %copy.41) | copy-start | bytes 6291460
  151.9 2.9 %copy-start.3 = (pred[256,256]{1,0:T(8,128)(4,1)S(1)}, pred[256,256]{1,0:T(8,128)(4,1)}, u32[]{:S(2)}) copy-start(pred[256,256]{1,0:T(8,128)(4,1)} %iota_compare_fusion) | copy-start | bytes 196612
  151.9 2.9 %copy-start.4 = (f32[32,256]{1,0:T(8,128)S(1)}, f32[32,256]{1,0:T(8,128)}, u32[]{:S(2)}) copy-start(f32[32,256]{1,0:T(8,128)} %bitcast_add_fusion.1) | copy-start | bytes 98308
  151.9 2.9 %copy-start.5 = (f32[1,256,32]{1,2,0:T(8,128)S(1)}, f32[1,256,32]{1,2,0:T(8,128)}, u32[]{:S(2)}) copy-start(f32[1,256,32]{1,2,0:T(8,128)} %copy.77) | copy-start | bytes 98308
  151.9 2.9 %copy-start.6 = (f32[1,32,256]{2,1,0:T(8,128)S(1)}, f32[1,32,256]{2,1,0:T(8,128)}, u32[]{:S(2)}) copy-start(f32[1,32,256]{2,1,0:T(8,128)} %copy.78) | copy-start | bytes 98308
  151.9 2.9 %copy-start.7 = (f32[32]{0:T(128)S(1)}, f32[32]{0:T(128)}, u32[]{:S(2)}) copy-start(f32[32]{0:T(128)} %param.9) | copy-start | bytes 388
where the time goes:
time: 162 us; the launch traced here: 161 us
  local copies, waits for them, and re-layouts  53.2 us (33%)
  other arithmetic  38.3 us (24%)
  blocking collectives  35 us (22%)
  starting transfers between devices  12.9 us (8%)
  matrix products  12.2 us (8%)
  waiting for transfers between devices  9.28 us (6%)
    all_gather x1, blocking collectives, carry_state(): all_logs = lax.all_gather(device_log[None, :], 'seq', axis=0, tiled=True)  35 us
    unnamed x2, other arithmetic  24.2 us
    convert_element_type x1, local copies, waits for them, and re-layouts, carry_state(): flat_state.astype(jnp.bfloat16)  17 us
    unnamed x23, local copies, waits for them, and re-layouts  9.99 us
    all_to_all x1, waiting for transfers between devices, carry_state(): lax.all_to_all(as_sent(mixed), 'seq', split_axis=0, concat_axis=1, tiled=...  9.28 us
    mul x3, local copies, waits for them, and re-layouts, group_terms(): weighted = (values * tail_weight[..., None]).astype(jnp.bfloat16)  7.62 us
    reshape x1, other arithmetic, on_device(): conv_activate(extended, conv_weight, row_count)  6.12 us
    convert_element_type x1, local copies, waits for them, and re-layouts, group_terms(): local_out = intra_out + skip_gain[:, None] * values.astype(jnp.float32)  5.6 us
  transfers between devices with their start and end apart: 3, of which 1 were waited for; matrix products, arithmetic and copies ran while one was open for 19% of the time, Pallas kernels for 0%

commit v1 on v0

--- a/solution.py
+++ b/solution.py
@@ -83,8 +83,14 @@
     head_count = device_log.shape[0]
     all_logs = lax.all_gather(device_log[None, :], "seq", axis=0, tiled=True)
     flat_state = final_state.reshape(1, head_count * HEADDIM, STATE)
-    received = lax.all_to_all(
-        flat_state.astype(jnp.bfloat16), "seq", split_axis=1, concat_axis=0, tiled=True
+    received = jnp.concatenate(
+        lax.all_to_all(
+            jnp.stack(jnp.split(flat_state.astype(jnp.bfloat16), lax.axis_size("seq"), axis=1)),
+            "seq",
+            0,
+            0,
+        ),
+        axis=0,
     ).astype(flat_state.dtype)
     source_count = received.shape[0]
     row_count = received.shape[1]

time: 162 us -> 124 us (0.77)
  other arithmetic: 38.3 us -> 14.7 us
  local copies, waits for them, and re-layouts: 53.2 us -> 39.4 us
    unnamed x2 -> x1, other arithmetic: 24.2 us -> 0.59 us
    convert_element_type x1 -> x0, local copies, waits for them, and re-layouts: 17 us -> none  [carry_state(): flat_state.astype(jnp.bfloat16)]
    unnamed x23 -> x34, local copies, waits for them, and re-layouts: 9.99 us -> 12.6 us
  transfers between devices with their start and end apart: 3 -> 3, of which waited for: 1 -> 1; matrix products, arithmetic and copies ran while one was open for 19% -> 25% of each run, Pallas kernels for 0% -> 0%
where the time goes in v1:
time: 124 us
  local copies, waits for them, and re-layouts  39.4 us (32%)
  blocking collectives  35 us (28%)
  other arithmetic  14.7 us (12%)
  starting transfers between devices  12.9 us (10%)
  matrix products  12.2 us (10%)
  waiting for transfers between devices  9.28 us (7%)
    all_gather x1, blocking collectives, carry_state(): all_logs = lax.all_gather(device_log[None, :], 'seq', axis=0, tiled=True)  35 us
    unnamed x34, local copies, waits for them, and re-layouts  12.6 us
    all_to_all x1, waiting for transfers between devices, carry_state(): lax.all_to_all(as_sent(mixed), 'seq', split_axis=0, concat_axis=1, tiled=...  9.27 us
    mul x3, local copies, waits for them, and re-layouts, group_terms(): weighted = (values * tail_weight[..., None]).astype(jnp.bfloat16)  7.62 us
    reshape x1, other arithmetic, on_device(): conv_activate(extended, conv_weight, row_count)  6.12 us
    convert_element_type x1, local copies, waits for them, and re-layouts, group_terms(): local_out = intra_out + skip_gain[:, None] * values.astype(jnp.float32)  5.6 us
    all_to_all x1, starting transfers between devices, carry_state(): lax.all_to_all(jnp.stack(jnp.split(flat_state.astype(jnp.bfloat16), lax.a...  5.1 us
    all_to_all x1, starting transfers between devices, carry_state(): lax.all_to_all(as_sent(mixed), 'seq', split_axis=0, concat_axis=1, tiled=...  4.14 us
  transfers between devices with their start and end apart: 3, of which 1 were waited for; matrix products, arithmetic and copies ran while one was open for 25% of the time, Pallas kernels for 0%

profile of v1, /device:TPU:9, one launch (start us, length us, event | category | flops | bytes accessed | tf_op | source)
XLA Modules:
  0.0 123.7 jit_solution(2300189016929561997)
XLA Ops:
  0.0 0.9 slice.46
  0.9 3.7 %collective-permute-start = (bf16[3,4352]{1,0:T(4,128)(2,1)S(1)}, bf16[3,4352]{1,0:T(4,128)(2,1)S(1)}, u32[]{:S(2)}, u32[]{:S(2)}) collective-permute-start(bf16[3,4352]{1,0:T(4,128)(2,1)S(1)} %slice.46), channel_id=1, source_target_pairs={{0,1},{1,2},{2,3},{3,4},{4,5},{5,6},{6,7},{7,8},{8,9},{9,10},{10,1... | collective-permute-start | bytes 78344 | tf_op jit(solution)/shard_map/ppermute | solution.py:22
  4.6 0.7 exponential_negate_fusion
  5.3 0.8 compare_select_fusion
  8.4 1.2 slice_reduce_fusion.4
  9.7 2.5 %mul.190 = f32[256,32,128]{2,1,0:T(8,128)} broadcast(f32[256,32]{1,0:T(8,128)S(1)} %bitcast.162), dimensions={0,1} | broadcast | bytes 4227072 | tf_op jit(solution)/shard_map/mul | solution.py:54
  12.3 5.0 %mul.191 = f32[1,256,4096]{2,1,0:T(8,128)} reshape(f32[256,32,128]{2,1,0:T(8,128)} %mul.190) | data formatting | bytes 8388608 | tf_op jit(solution)/shard_map/mul | solution.py:54
  17.3 6.1 %fusion.13 = bf16[1,256,4352]{2,1,0:T(8,128)(2,1)S(1)} fusion(bf16[256,4352]{1,0:T(8,128)(2,1)} %param.5, f32[4352]{0:T(1024)S(1)} %get-tuple-element.27, bf16[3,4352]{1,0:T(4,128)(2,1)S(1)} %collective-permute-done, f32[4352]{0:T(1024)S(1)} %get-tuple-element.28, f32[4352]{0:T(1024)S(1)} %get-tuple-element.26, f32[4352]{0:T(1024)S(1)} %get-tuple-element.20), kind=kLoop, calls=%fused_computation.21 | loop fusion | flops 27852800 | bytes 4552192 | tf_op jit(solution)/shard_map/reshape | solution.py:124
  24.5 3.0 %fusion.1 = bf16[1,4096,128]{2,1,0:T(8,128)(2,1)S(1)} fusion(bf16[32,8,32,128]{3,2,1,0:T(8,128)(2,1)S(1)} %copy.47, f32[4096]{0:T(1024)S(1)} %broadcast_bitcast_fusion, bf16[1,256,4352]{2,1,0:T(8,128)(2,1)S(1)} %fusion.13), kind=kOutput, calls=%fused_computation.3 | convolution fusion | flops 269484032 | bytes 3227648 | tf_op jit(solution)/shard_map/cshp,csn->chpn/dot_general | solution.py:55
  27.5 0.6 fusion.53
  28.1 0.6 fusion.52
  28.8 0.6 fusion.51
  29.4 0.6 fusion.50
  30.0 0.6 fusion.49
  37.0 0.6 fusion.38
  37.6 5.1 %all-to-all-start = ((bf16[16,1,256,128]{3,2,1,0:T(8,128)(2,1)}), bf16[16,1,256,128]{3,2,1,0:T(8,128)(2,1)S(1)}, u32[]{:S(2)}, u32[]{:S(2)}) async-start(bf16[16,1,256,128]{3,2,1,0:T(8,128)(2,1)} %fusion.38), calls=%async_computation | async-start | bytes 2097152 | tf_op jit(solution)/shard_map/all_to_all | solution.py:87
  42.8 35.0 %all-gather = f32[16,1,32]{2,1,0:T(1,128)S(1)} all-gather(f32[1,1,32]{2,1,0:T(1,128)S(1)} %copy.35), channel_id=2, replica_groups=mesh['grp'=2,'seq'=16] {'seq'}, dimensions={0}, use_global_device_ids=true | all-gather | bytes 2176 | tf_op jit(solution)/shard_map/all_gather | solution.py:84
  78.8 1.5 %copy.36 = f32[16,256]{0,1:T(8,128)} copy(f32[16,256]{1,0:T(8,128)} %sub.66) | data formatting | bytes 32768 | tf_op jit(solution)/shard_map/sub | solution.py:104
  80.3 3.9 %fusion.24 = bf16[16,256,128]{2,0,1:T(8,128)(2,1)S(1)} fusion(bf16[16,256,128]{2,1,0:T(8,128)(2,1)S(1)} %bitcast.161, f32[16,256]{0,1:T(8,128)S(1)} %copy.37, f32[16,256]{0,1:T(8,128)} %copy.36, pred[16,16]{1,0:T(8,128)(4,1)S(1)} %iota_compare_fusion.3), kind=kOutput, calls=%fused_computation.31 | convolution fusion | flops 101318656 | bytes 2130176 | tf_op jit(solution)/shard_map/sjr,jrn->srn/dot_general | solution.py:110
  84.3 1.2 %copy.39 = bf16[16,256,128]{2,1,0:T(8,128)(2,1)} copy(bf16[16,256,128]{2,0,1:T(8,128)(2,1)S(1)} %fusion.24) | data formatting | bytes 2097152 | tf_op jit(solution)/shard_map/convert_element_type | solution.py:14
  85.5 4.1 %all-to-all-start.1 = ((bf16[16,256,128]{2,1,0:T(8,128)(2,1)}), bf16[16,256,128]{2,1,0:T(8,128)(2,1)S(1)}, u32[]{:S(2)}, u32[]{:S(2)}) async-start(bf16[16,256,128]{2,1,0:T(8,128)(2,1)} %copy.39), calls=%async_computation.1 | async-start | bytes 2097152 | tf_op jit(solution)/shard_map/all_to_all | solution.py:111
  90.9 0.6 iota_compare_fusion
  92.2 3.2 %fusion.64 = (bf16[1,256,4096]{2,1,0:T(8,128)(2,1)}, f32[1,256,4096]{2,1,0:T(8,128)}) fusion(bf16[1,256,4352]{2,1,0:T(8,128)(2,1)S(1)} %fusion.13), kind=kLoop, calls=%fused_computation.112 | loop fusion | flops 1048576 | bytes 8388608 | tf_op jit(solution)/shard_map/slice | solution.py:39
  95.4 4.1 %copy.28 = bf16[1,256,4096]{1,2,0:T(8,128)(2,1)} copy(bf16[1,256,4096]{2,1,0:T(8,128)(2,1)} %get-tuple-element.36) | data formatting | bytes 4194304 | tf_op jit(solution)/shard_map/slice | solution.py:39
  99.4 5.6 %copy.32 = f32[1,256,4096]{1,2,0:T(8,128)} copy(f32[1,256,4096]{2,1,0:T(8,128)} %get-tuple-element.38) | data formatting | bytes 8388608 | tf_op jit(solution)/shard_map/convert_element_type | solution.py:52
  105.2 9.3 %all-to-all-done.1 = bf16[16,256,128]{2,1,0:T(8,128)(2,1)S(1)} async-done(((bf16[16,256,128]{2,1,0:T(8,128)(2,1)}), bf16[16,256,128]{2,1,0:T(8,128)(2,1)S(1)}, u32[]{:S(2)}, u32[]{:S(2)}) %all-to-all-start.1) | async-done | bytes 1048608 | tf_op jit(solution)/shard_map/all_to_all | solution.py:111
  114.5 0.7 fusion.28
  115.3 0.7 fusion.30
  116.0 0.7 copy-done.1
  116.7 0.7 copy-done.2
  117.4 3.4 %fusion.4 = bf16[1,256,32,128]{1,3,2,0:T(8,128)(2,1)S(1)} fusion(f32[256,32,128]{0,2,1:T(8,128)S(1)} %fusion.30, f32[256,32,128]{0,2,1:T(8,128)S(1)} %fusion.28, f32[1,256,32,128]{1,3,2,0:T(8,128)S(1)} %bitcast.158, f32[256,32]{0,1:T(8,128)S(1)} %bitcast.169, f32[32]{0:T(128)S(1)} %copy-done.7, bf16[256,32,128]{0,2,1:T(8,128)(2,1)S(1)} %bitcast.159, ...), kind=kOutput, calls=%fused_computation.8 | convolution fusion | flops 553648128 | bytes 17203328 | tf_op jit(solution)/shard_map/chqs,cshp->cqhp/dot_general | solution.py:51
  120.8 2.9 %copy.40 = bf16[256,4096]{1,0:T(8,128)(2,1)} copy(bf16[256,4096]{0,1:T(8,128)(2,1)S(1)} %bitcast.160) | data formatting | bytes 4194304 | tf_op jit(solution)/shard_map/convert_element_type | solution.py:136
  (55 shorter events, 12.9 us)
Async XLA Ops:
  0.9 16.4 %collective-permute-start = (bf16[3,4352]{1,0:T(4,128)(2,1)S(1)}, bf16[3,4352]{1,0:T(4,128)(2,1)S(1)}, u32[]{:S(2)}, u32[]{:S(2)}) collective-permute-start(bf16[3,4352]{1,0:T(4,128)(2,1)S(1)} %slice.46), channel_id=1, source_target_pairs={{0,1},{1,2},{2,3},{3,4},{4,5},{5,6},{6,7},{7,8},{8,9},{9,10},{10,1... | collective-permute-start | bytes 78344 | tf_op jit(solution)/shard_map/ppermute | solution.py:22
  17.3 6.1 %copy-start = (f32[1,256,4096]{2,1,0:T(8,128)S(1)}, f32[1,256,4096]{2,1,0:T(8,128)}, u32[]{:S(2)}) copy-start(f32[1,256,4096]{2,1,0:T(8,128)} %mul.191) | copy-start | bytes 12582916
  37.6 42.7 %all-to-all-start = ((bf16[16,1,256,128]{3,2,1,0:T(8,128)(2,1)}), bf16[16,1,256,128]{3,2,1,0:T(8,128)(2,1)S(1)}, u32[]{:S(2)}, u32[]{:S(2)}) async-start(bf16[16,1,256,128]{3,2,1,0:T(8,128)(2,1)} %fusion.38), calls=%async_computation | async-start | bytes 2097152 | tf_op jit(solution)/shard_map/all_to_all | solution.py:87
  85.5 29.0 %all-to-all-start.1 = ((bf16[16,256,128]{2,1,0:T(8,128)(2,1)}), bf16[16,256,128]{2,1,0:T(8,128)(2,1)S(1)}, u32[]{:S(2)}, u32[]{:S(2)}) async-start(bf16[16,256,128]{2,1,0:T(8,128)(2,1)} %copy.39), calls=%async_computation.1 | async-start | bytes 2097152 | tf_op jit(solution)/shard_map/all_to_all | solution.py:111
  114.5 2.2 %copy-start.1 = (f32[1,256,4096]{1,2,0:T(8,128)S(1)}, f32[1,256,4096]{1,2,0:T(8,128)}, u32[]{:S(2)}) copy-start(f32[1,256,4096]{1,2,0:T(8,128)} %copy.32) | copy-start | bytes 12582916
  114.5 2.9 %copy-start.2 = (bf16[1,256,4096]{1,2,0:T(8,128)(2,1)S(1)}, bf16[1,256,4096]{1,2,0:T(8,128)(2,1)}, u32[]{:S(2)}) copy-start(bf16[1,256,4096]{1,2,0:T(8,128)(2,1)} %copy.28) | copy-start | bytes 6291460
  114.5 2.9 %copy-start.3 = (pred[256,256]{1,0:T(8,128)(4,1)S(1)}, pred[256,256]{1,0:T(8,128)(4,1)}, u32[]{:S(2)}) copy-start(pred[256,256]{1,0:T(8,128)(4,1)} %iota_compare_fusion) | copy-start | bytes 196612
  114.5 2.9 %copy-start.4 = (f32[32,256]{1,0:T(8,128)S(1)}, f32[32,256]{1,0:T(8,128)}, u32[]{:S(2)}) copy-start(f32[32,256]{1,0:T(8,128)} %bitcast_add_fusion.1) | copy-start | bytes 98308
  114.5 2.9 %copy-start.5 = (f32[1,256,32]{1,2,0:T(8,128)S(1)}, f32[1,256,32]{1,2,0:T(8,128)}, u32[]{:S(2)}) copy-start(f32[1,256,32]{1,2,0:T(8,128)} %copy.61) | copy-start | bytes 98308
  114.5 2.9 %copy-start.6 = (f32[1,32,256]{2,1,0:T(8,128)S(1)}, f32[1,32,256]{2,1,0:T(8,128)}, u32[]{:S(2)}) copy-start(f32[1,32,256]{2,1,0:T(8,128)} %copy.62) | copy-start | bytes 98308
  114.5 2.9 %copy-start.7 = (f32[32]{0:T(128)S(1)}, f32[32]{0:T(128)}, u32[]{:S(2)}) copy-start(f32[32]{0:T(128)} %param.9) | copy-start | bytes 388
